TPU v7x, 32 devices: a whole 2x2x4 slice. The times are simulated.
32 devices in a mesh: ctx: 4 (over z), exp: 8 (over y, x, core).
Axes of the slice: x: 2, y: 2, z: 4, core: 2. Of those that a mesh axis runs over, the one named last changes fastest.
Arguments:
- out_grad: bfloat16 [4096, 2048], P(('ctx', 'exp')), may hold values from -6 to 6
- route_ids: int32 [4096, 4], P(('ctx', 'exp')), may hold values from 0 to 15, all different within a row; in each aligned block of 128 rows (0 to 127, 128 to 255, ...) at most 36 rows name the same one
- gate_probs: float32 [4096, 4], P(('ctx', 'exp')), may hold values from 0 to 1, as said below
- saved_hidden: bfloat16 [4, 8, 16, 36, 768], P('ctx', None, 'exp'), may hold values from -6 to 6
- down_weight: bfloat16 [16, 768, 2048], P('exp', None, 'ctx'), may hold values from -0.02734375 to 0.02734375
- router_weight: bfloat16 [2048, 16], replicated, may hold values from -1.5 to 1.5
- proj_weight: bfloat16 [4096, 2048], P('ctx'), may hold values from -0.125 to 0.125
Outputs:
- head_grads: bfloat16 [4, 1024, 4096], P(None, 'exp', 'ctx')
- router_grad: float32 [4096, 4], P(('ctx', 'exp'))
Inputs may be any that keep to these rules, and one draw needn't show every extreme that they name: `route_ids`: each token names 4 different experts; among the tokens of one device no expert is named more than 36 times, and in some device some expert is named exactly 36 times. `gate_probs`: positive; a token's 4 gates sum to one.
All inputs are finite; a program needn't handle non-finite values.
Results may differ from a plain program's by a relative error of at most 0.009.
Values may be sent and summed in bfloat16 or wider, within the bound.
A program may use at most 64 MiB of HBM per device.

v0:
```python
import jax
import jax.numpy as jnp
from jax import lax
from jax.sharding import PartitionSpec as P


def route_ranks(route_ids, experts):
    flat_ids = route_ids.reshape(-1)
    onehot = (flat_ids[:, None] == jnp.arange(experts, dtype=jnp.int32)[None, :]).astype(jnp.int32)
    earlier = jnp.cumsum(onehot, axis=0) - onehot
    slot_rank = jnp.sum(earlier * onehot, axis=1)
    return (flat_ids, slot_rank)


def shards(out_grad, route_ids, gate_probs, saved_hidden, down_weight, router_weight, proj_weight):
    tok_rows, top_count = route_ids.shape
    experts = router_weight.shape[1]
    groups = lax.axis_size("exp")
    local_experts = down_weight.shape[0]
    capacity = saved_hidden.shape[3]
    arrived_rows = lax.all_gather(out_grad, "ctx", axis=0, tiled=True)
    flat_ids, slot_rank = route_ranks(route_ids, experts)
    positions = flat_ids * capacity + slot_rank
    hidden_local = saved_hidden[0]
    spread = jnp.repeat(out_grad, top_count, axis=0)
    send_rows = (
        jnp.zeros((experts * capacity, out_grad.shape[1]), out_grad.dtype).at[positions].set(spread)
    )
    send_rows = send_rows.reshape(groups, local_experts, capacity, out_grad.shape[1])
    arrived = lax.all_to_all(send_rows, "exp", split_axis=0, concat_axis=0, tiled=True)
    outputs = jnp.einsum(
        "secf,efn->secn",
        hidden_local,
        lax.all_gather(down_weight, "ctx", axis=2, tiled=True),
        preferred_element_type=jnp.float32,
    ).astype(jnp.bfloat16)
    partial_grad = jnp.sum(arrived.astype(jnp.float32) * outputs.astype(jnp.float32), axis=3)
    returned = lax.all_to_all(partial_grad, "exp", split_axis=0, concat_axis=0, tiled=True)
    gate_grad = returned.reshape(-1)[positions].reshape(tok_rows, top_count)
    weighted = jnp.sum(gate_probs * gate_grad, axis=1, keepdims=True)
    router_grad = gate_probs * (gate_grad - weighted)
    matches = route_ids[:, :, None] == jnp.arange(experts, dtype=jnp.int32)[None, None, :]
    dense_grad = jnp.sum(jnp.where(matches, router_grad[:, :, None], 0.0), axis=1)
    router_wide = router_weight.astype(jnp.float32)
    dense_all = lax.all_gather(dense_grad.astype(jnp.bfloat16), "ctx", axis=0, tiled=True).astype(
        dense_grad.dtype
    )
    combined = (
        arrived_rows.astype(jnp.float32)
        + lax.dot_general(
            dense_all, router_wide, (((1,), (1,)), ((), ())), precision=lax.Precision.HIGHEST
        )
    ).astype(jnp.bfloat16)
    head_flat = lax.dot_general(
        combined, proj_weight, (((1,), (1,)), ((), ())), preferred_element_type=jnp.float32
    ).astype(jnp.bfloat16)
    head_grads = head_flat.reshape(lax.axis_size("ctx"), tok_rows, proj_weight.shape[0])
    return (head_grads, router_grad)


def solution(mesh):
    return jax.shard_map(
        shards,
        mesh=mesh,
        in_specs=(
            P(("ctx", "exp"), None),
            P(("ctx", "exp"), None),
            P(("ctx", "exp"), None),
            P("ctx", None, "exp", None, None),
            P("exp", None, "ctx"),
            P(),
            P("ctx", None),
        ),
        out_specs=(P(None, "exp", "ctx"), P(("ctx", "exp"), None)),
        check_vma=False,
    )
```

profile of v0, /device:TPU:0, one launch (start us, length us, event | category | flops | bytes accessed | tf_op | source)
XLA Modules:
  0.0 186.4 jit_solution(17179931395707088919)
XLA Ops:
  7.2 0.7 all-gather.5.cloned.1.call-update
  7.9 0.8 copy.58
  8.7 0.1 eq.45
  8.8 0.1 eq.41
  8.9 1.2 reduce-window.6
  10.1 0.2 slice_reduce_fusion
  10.4 0.7 broadcast_multiply_fusion
  11.0 0.1 copy.57
  11.2 0.1 mul.30
  11.3 1.0 broadcast_in_dim.26
  12.3 2.1 %reshape.86 = bf16[512,2048]{1,0:T(8,128)(2,1)} reshape(bf16[128,4,2048]{2,1,0:T(4,128)(2,1)S(1)} %broadcast_in_dim.26) | data formatting | bytes 4194304 | tf_op jit(solution)/shard_map/reshape | solution.py:25
  14.5 0.1 fusion.13
  14.6 6.3 %scatter_custom_fusion = bf16[576,2048]{1,0:T(8,128)(2,1)} fusion(s32[512]{0:T(512)S(1)} %bitcast.41, bf16[512,2048]{1,0:T(8,128)(2,1)} %reshape.86, bf16[]{:T(256)} %constant.5.clone.1), kind=kCustom, calls=%fused_computation.9 | custom fusion | bytes 2359808 | tf_op jit(solution)/shard_map/scatter | solution.py:27
  20.9 2.7 %reshape.70 = bf16[8,2,36,2048]{3,2,1,0:T(8,128)(2,1)S(1)} reshape(bf16[576,2048]{1,0:T(8,128)(2,1)} %scatter_custom_fusion) | data formatting | bytes 4718592 | tf_op jit(solution)/shard_map/reshape | solution.py:29
  23.6 3.9 %copy.61 = bf16[8,2,36,2048]{3,1,2,0:T(2,128)(2,1)} copy(bf16[8,2,36,2048]{3,2,1,0:T(8,128)(2,1)S(1)} %reshape.70) | data formatting | bytes 4718592 | tf_op jit(solution)/shard_map/reshape | solution.py:29
  27.5 5.2 %all-to-all-start = ((bf16[8,2,36,2048]{3,1,2,0:T(2,128)(2,1)}), bf16[8,2,36,2048]{3,1,2,0:T(2,128)(2,1)S(1)}, u32[]{:S(2)}, u32[]{:S(2)}) async-start(bf16[8,2,36,2048]{3,1,2,0:T(2,128)(2,1)} %copy.61), calls=%async_computation | async-start | bytes 4718592 | tf_op jit(solution)/shard_map/all_to_all | solution.py:30
  32.7 0.7 all-gather.3.cloned.1.call-update
  33.4 28.7 %all-to-all-done = bf16[8,2,36,2048]{3,1,2,0:T(2,128)(2,1)S(1)} async-done(((bf16[8,2,36,2048]{3,1,2,0:T(2,128)(2,1)}), bf16[8,2,36,2048]{3,1,2,0:T(2,128)(2,1)S(1)}, u32[]{:S(2)}, u32[]{:S(2)}) %all-to-all-start) | async-done | bytes 2359328 | tf_op jit(solution)/shard_map/all_to_all | solution.py:30
  62.1 65.6 %all-gather.5.cloned.1.call-done = bf16[2,768,2048]{2,1,0:T(8,128)(2,1)} async-done(((bf16[2,768,512]{2,1,0:T(8,128)(2,1)}), bf16[2,768,2048]{2,1,0:T(8,128)(2,1)}) %all-gather.5.cloned.1.call-update) | async-done | bytes 6291472 | tf_op jit(solution)/shard_map/all_gather | solution.py:34
  127.7 6.1 %fusion.2 = f32[8,2,36]{2,0,1:T(8,128)S(1)} fusion(bf16[8,2,36,2048]{3,1,2,0:T(2,128)(2,1)S(1)} %all-to-all-done, bf16[2,768,2048]{2,1,0:T(8,128)(2,1)} %all-gather.5.cloned.1.call-done, bf16[8,2,36,768]{3,1,2,0:T(2,128)(2,1)S(1)} %bitcast.40), kind=kOutput, calls=%fused_computation.5 | convolution fusion | flops 1817837056 | bytes 9537792 | tf_op jit(solution)/shard_map/secf,efn->secn/dot_general | solution.py:31
  133.8 0.6 copy.64
  134.4 3.8 %all-to-all-start.1 = ((f32[8,2,36]{2,1,0:T(2,128)}), f32[8,2,36]{2,1,0:T(2,128)S(1)}, u32[]{:S(2)}, u32[]{:S(2)}) async-start(f32[8,2,36]{2,1,0:T(2,128)} %copy.64), calls=%async_computation.1 | async-start | bytes 16384 | tf_op jit(solution)/shard_map/all_to_all | solution.py:38
  138.3 0.1 copy.66
  138.4 4.6 %all-to-all-done.1 = f32[8,2,36]{2,1,0:T(2,128)S(1)} async-done(((f32[8,2,36]{2,1,0:T(2,128)}), f32[8,2,36]{2,1,0:T(2,128)S(1)}, u32[]{:S(2)}, u32[]{:S(2)}) %all-to-all-start.1) | async-done | bytes 2336 | tf_op jit(solution)/shard_map/all_to_all | solution.py:38
  143.1 2.3 %gather_fusion = f32[512]{0:T(512)S(1)} fusion(f32[576]{0:T(1024)S(1)} %reshape.71, s32[1024]{0:T(1024)S(1)} %pad_clamp_fusion), kind=kCustom, calls=%fused_computation | custom fusion | bytes 6144 | tf_op jit(solution)/shard_map/gather | solution.py:39
  145.3 0.1 reshape.72
  145.5 0.1 multiply_reduce_fusion
  145.8 12.6 %all_gather.11 = bf16[512,16]{0,1:T(8,128)(2,1)S(1)} all-gather(bf16[128,16]{0,1:T(8,128)(2,1)S(1)} %select_reduce_fusion), channel_id=1, replica_groups=mesh['ctx'=4,'exp'=8] {'ctx'}, dimensions={0}, use_global_device_ids=true | all-gather | bytes 20480 | tf_op jit(solution)/shard_map/all_gather | solution.py:45
  158.4 15.0 %all-gather.3.cloned.1.call-done = bf16[512,2048]{1,0:T(8,128)(2,1)} async-done(((bf16[128,2048]{1,0:T(8,128)(2,1)}), bf16[512,2048]{1,0:T(8,128)(2,1)}) %all-gather.3.cloned.1.call-update) | async-done | bytes 2097168 | tf_op jit(solution)/shard_map/all_gather | solution.py:21
  173.4 2.5 %add_convert_fusion = bf16[512,2048]{1,0:T(8,128)(2,1)S(1)} fusion(bf16[512,2048]{1,0:T(8,128)(2,1)} %all-gather.3.cloned.1.call-done, bf16[512,16]{0,1:T(8,128)(2,1)S(1)} %all_gather.11, bf16[2048,16]{0,1:T(8,128)(2,1)S(1)} %copy-done.2), kind=kOutput, calls=%fused_computation.6 | convolution fusion | flops 36700160 | bytes 4276224 | tf_op jit(solution)/shard_map/dot_general | solution.py:50
  175.8 0.3 copy-done.6
  176.2 3.3 %convolution_convert_fusion = bf16[512,1024]{1,0:T(8,128)(2,1)} fusion(bf16[512,2048]{1,0:T(8,128)(2,1)S(1)} %add_convert_fusion, bf16[1024,2048]{1,0:T(8,128)(2,1)S(1)} %copy-done.6), kind=kOutput, calls=%fused_computation.8 | convolution fusion | flops 2148007936 | bytes 7340032 | tf_op jit(solution)/shard_map/dot_general | solution.py:54
  (24 shorter events, 0.4 us)
Async XLA Ops:
  7.2 120.5 %copy-start = (bf16[1,8,2,36,768]{4,2,3,1,0:T(2,128)(2,1)S(1)}, bf16[1,8,2,36,768]{4,2,3,1,0:T(2,128)(2,1)}, u32[]{:S(2)}) copy-start(bf16[1,8,2,36,768]{4,2,3,1,0:T(2,128)(2,1)} %param.10) | copy-start | bytes 2654212
  7.2 4.1 %copy-start.1 = (bf16[128,2048]{1,0:T(8,128)(2,1)S(1)}, bf16[128,2048]{1,0:T(8,128)(2,1)}, u32[]{:S(2)}) copy-start(bf16[128,2048]{1,0:T(8,128)(2,1)} %param.7) | copy-start | bytes 1572868
  7.2 120.5 %all-gather.5.cloned.1.call-start = ((), (), s32[]{:S(2)}) async-start(), calls=%async_computation.3 | async-start | bytes 7864320 | tf_op jit(solution)/shard_map/all_gather | solution.py:34
  27.5 34.6 %all-to-all-start = ((bf16[8,2,36,2048]{3,1,2,0:T(2,128)(2,1)}), bf16[8,2,36,2048]{3,1,2,0:T(2,128)(2,1)S(1)}, u32[]{:S(2)}, u32[]{:S(2)}) async-start(bf16[8,2,36,2048]{3,1,2,0:T(2,128)(2,1)} %copy.61), calls=%async_computation | async-start | bytes 4718592 | tf_op jit(solution)/shard_map/all_to_all | solution.py:30
  32.7 140.7 %all-gather.3.cloned.1.call-start = ((), (), s32[]{:S(2)}) async-start(), calls=%async_computation.2 | async-start | bytes 2621440 | tf_op jit(solution)/shard_map/all_gather | solution.py:21
  127.7 10.6 %copy-start.5 = (f32[128,4]{0,1:T(4,128)S(1)}, f32[128,4]{0,1:T(4,128)}, u32[]{:S(2)}) copy-start(f32[128,4]{0,1:T(4,128)} %param.9) | copy-start | bytes 6148
  133.8 11.9 %copy-start.3 = (s32[128,4]{0,1:T(4,128)S(1)}, s32[128,4]{0,1:T(4,128)}, u32[]{:S(2)}) copy-start(s32[128,4]{0,1:T(4,128)} %param.8) | copy-start | bytes 6148
  133.8 39.6 %copy-start.2 = (bf16[2048,16]{0,1:T(8,128)(2,1)S(1)}, bf16[2048,16]{0,1:T(8,128)(2,1)}, u32[]{:S(2)}) copy-start(bf16[2048,16]{0,1:T(8,128)(2,1)} %param.12) | copy-start | bytes 196612
  134.4 8.5 %all-to-all-start.1 = ((f32[8,2,36]{2,1,0:T(2,128)}), f32[8,2,36]{2,1,0:T(2,128)S(1)}, u32[]{:S(2)}, u32[]{:S(2)}) async-start(f32[8,2,36]{2,1,0:T(2,128)} %copy.64), calls=%async_computation.1 | async-start | bytes 16384 | tf_op jit(solution)/shard_map/all_to_all | solution.py:38
  145.7 33.8 %copy-start.4 = (f32[128,4]{0,1:T(4,128)}, f32[128,4]{0,1:T(4,128)S(1)}, u32[]{:S(2)}) copy-start(f32[128,4]{0,1:T(4,128)S(1)} %copy.67) | copy-start | bytes 6148
  173.4 2.8 %copy-start.6 = (bf16[1024,2048]{1,0:T(8,128)(2,1)S(1)}, bf16[1024,2048]{1,0:T(8,128)(2,1)}, u32[]{:S(2)}) copy-start(bf16[1024,2048]{1,0:T(8,128)(2,1)} %param.13) | copy-start | bytes 12582916
Sparse Core Ops, SparseCore 0:
  9.6 118.0 all-gather.4
  129.2 44.0 all-gather.2
where the time goes:
time: 187 us; the launch traced here: 186 us
  waiting for transfers between devices  115 us (61%)
  local copies, waits for them, and re-layouts  21.1 us (11%)
  between operations  14.2 us (8%)
  blocking collectives  12.6 us (7%)
  matrix products  11.9 us (6%)
  starting transfers between devices  9.12 us (5%)
  other arithmetic  2.22 us (1%)
    all_gather x1, waiting for transfers between devices, shards(): lax.all_gather(down_weight, 'ctx', axis=2, tiled=True)  65.6 us
    all_to_all x1, waiting for transfers between devices, shards(): lax.all_to_all(send_rows, 'exp', split_axis=0, concat_axis=0, tiled=True)  28.7 us
    all_gather x1, waiting for transfers between devices, shards(): arrived_rows = lax.all_gather(out_grad, 'ctx', axis=0, tiled=True)  15 us
    all_gather x1, blocking collectives, shards(): lax.all_gather(dense_grad.astype(jnp.bfloat16), 'ctx', axis=0, tiled=True)  12.6 us
    reshape x2, local copies, waits for them, and re-layouts, shards(): send_rows.reshape(groups, local_experts, capacity, out_grad.shape[1])  6.6 us
    scatter x1, local copies, waits for them, and re-layouts, shards(): jnp.zeros((experts * capacity, out_grad.shape[1]), out_grad.dtype)  6.29 us
    dot_general x1, matrix products, shards(): jnp.einsum('secf,efn->secn', hidden_local, lax.all_gather(down_weight, 'c...  6.13 us
    all_to_all x1, starting transfers between devices, shards(): lax.all_to_all(send_rows, 'exp', split_axis=0, concat_axis=0, tiled=True)  5.21 us
  transfers between devices with their start and end apart: 4, of which 4 were waited for; matrix products, arithmetic and copies ran while one was open for 16% of the time, Pallas kernels for 0%

commit v1 on v0

--- a/solution.py
+++ b/solution.py
@@ -42,9 +42,15 @@
     matches = route_ids[:, :, None] == jnp.arange(experts, dtype=jnp.int32)[None, None, :]
     dense_grad = jnp.sum(jnp.where(matches, router_grad[:, :, None], 0.0), axis=1)
     router_wide = router_weight.astype(jnp.float32)
-    dense_all = lax.all_gather(dense_grad.astype(jnp.bfloat16), "ctx", axis=0, tiled=True).astype(
-        dense_grad.dtype
-    )
+    dense_all = jnp.concatenate(
+        lax.all_to_all(
+            jnp.stack(lax.axis_size("ctx") * [dense_grad.astype(jnp.bfloat16)], axis=0),
+            axis_name="ctx",
+            split_axis=0,
+            concat_axis=0,
+        ),
+        axis=0,
+    ).astype(dense_grad.dtype)
     combined = (
         arrived_rows.astype(jnp.float32)
         + lax.dot_general(

time: 187 us -> 187 us (level)
  blocking collectives: 12.6 us -> 0 us
  waiting for transfers between devices: 115 us -> 124 us
  starting transfers between devices: 9.12 us -> 12.4 us
    all_gather x1 -> x0, blocking collectives: 12.6 us -> none  [shards(): lax.all_gather(dense_grad.astype(jnp.bfloat16), 'ctx', axis=0, tiled=True)]
    all_gather x1, waiting for transfers between devices: 15 us -> 23.6 us  [shards(): arrived_rows = lax.all_gather(out_grad, 'ctx', axis=0, tiled=True)]
    all_to_all x0 -> x1, starting transfers between devices: none -> 3.25 us  [shards(): lax.all_to_all(jnp.stack(lax.axis_size('ctx') * [dense_grad.astype(jnp.bf...]
  transfers between devices with their start and end apart: 4 -> 5, of which waited for: 4 -> 4; matrix products, arithmetic and copies ran while one was open for 16% -> 16% of each run, Pallas kernels for 0% -> 0%
where the time goes in v1:
time: 187 us; the launch traced here: 186 us
  waiting for transfers between devices  124 us (66%)
  local copies, waits for them, and re-layouts  21.7 us (12%)
  between operations  14.2 us (8%)
  starting transfers between devices  12.4 us (7%)
  matrix products  12.1 us (6%)
  other arithmetic  2.22 us (1%)
    all_gather x1, waiting for transfers between devices, shards(): lax.all_gather(down_weight, 'ctx', axis=2, tiled=True)  65.6 us
    all_to_all x1, waiting for transfers between devices, shards(): lax.all_to_all(send_rows, 'exp', split_axis=0, concat_axis=0, tiled=True)  28.7 us
    all_gather x1, waiting for transfers between devices, shards(): arrived_rows = lax.all_gather(out_grad, 'ctx', axis=0, tiled=True)  23.6 us
    reshape x2, local copies, waits for them, and re-layouts, shards(): send_rows.reshape(groups, local_experts, capacity, out_grad.shape[1])  6.6 us
    dot_general x1, matrix products, shards(): jnp.einsum('secf,efn->secn', hidden_local, lax.all_gather(down_weight, 'c...  6.34 us
    scatter x1, local copies, waits for them, and re-layouts, shards(): jnp.zeros((experts * capacity, out_grad.shape[1]), out_grad.dtype)  6.29 us
    all_to_all x1, starting transfers between devices, shards(): lax.all_to_all(send_rows, 'exp', split_axis=0, concat_axis=0, tiled=True)  5.2 us
    all_to_all x1, waiting for transfers between devices, shards(): lax.all_to_all(partial_grad, 'exp', split_axis=0, concat_axis=0, tiled=True)  4.58 us
  transfers between devices with their start and end apart: 5, of which 4 were waited for; matrix products, arithmetic and copies ran while one was open for 16% of the time, Pallas kernels for 0%

profile of v1, /device:TPU:0, one launch (start us, length us, event | category | flops | bytes accessed | tf_op | source)
XLA Modules:
  0.0 186.4 jit_solution(17586530756035697667)
XLA Ops:
  7.2 0.7 all-gather.5.cloned.1.call-update
  7.9 0.8 copy.60
  8.7 0.1 eq.45
  8.8 0.1 eq.41
  8.9 1.2 reduce-window.6
  10.1 0.2 slice_reduce_fusion
  10.4 0.7 broadcast_multiply_fusion
  11.0 0.1 copy.59
  11.2 0.1 mul.30
  11.3 1.0 broadcast_in_dim.26
  12.3 2.1 %reshape.92 = bf16[512,2048]{1,0:T(8,128)(2,1)} reshape(bf16[128,4,2048]{2,1,0:T(4,128)(2,1)S(1)} %broadcast_in_dim.26) | data formatting | bytes 4194304 | tf_op jit(solution)/shard_map/reshape | solution.py:25
  14.6 6.3 %scatter_custom_fusion = bf16[576,2048]{1,0:T(8,128)(2,1)} fusion(s32[512]{0:T(512)S(1)} %bitcast.47, bf16[512,2048]{1,0:T(8,128)(2,1)} %reshape.92, bf16[]{:T(256)} %constant.5.clone.1), kind=kCustom, calls=%fused_computation.9 | custom fusion | bytes 2359808 | tf_op jit(solution)/shard_map/scatter | solution.py:27
  20.8 2.7 %reshape.75 = bf16[8,2,36,2048]{3,2,1,0:T(8,128)(2,1)S(1)} reshape(bf16[576,2048]{1,0:T(8,128)(2,1)} %scatter_custom_fusion) | data formatting | bytes 4718592 | tf_op jit(solution)/shard_map/reshape | solution.py:29
  23.6 3.8 %copy.63 = bf16[8,2,36,2048]{3,1,2,0:T(2,128)(2,1)} copy(bf16[8,2,36,2048]{3,2,1,0:T(8,128)(2,1)S(1)} %reshape.75) | data formatting | bytes 4718592 | tf_op jit(solution)/shard_map/reshape | solution.py:29
  27.5 5.2 %all-to-all-start = ((bf16[8,2,36,2048]{3,1,2,0:T(2,128)(2,1)}), bf16[8,2,36,2048]{3,1,2,0:T(2,128)(2,1)S(1)}, u32[]{:S(2)}, u32[]{:S(2)}) async-start(bf16[8,2,36,2048]{3,1,2,0:T(2,128)(2,1)} %copy.63), calls=%async_computation | async-start | bytes 4718592 | tf_op jit(solution)/shard_map/all_to_all | solution.py:30
  32.7 0.7 all-gather.3.cloned.1.call-update
  33.4 28.7 %all-to-all-done = bf16[8,2,36,2048]{3,1,2,0:T(2,128)(2,1)S(1)} async-done(((bf16[8,2,36,2048]{3,1,2,0:T(2,128)(2,1)}), bf16[8,2,36,2048]{3,1,2,0:T(2,128)(2,1)S(1)}, u32[]{:S(2)}, u32[]{:S(2)}) %all-to-all-start) | async-done | bytes 2359328 | tf_op jit(solution)/shard_map/all_to_all | solution.py:30
  62.1 65.6 %all-gather.5.cloned.1.call-done = bf16[2,768,2048]{2,1,0:T(8,128)(2,1)} async-done(((bf16[2,768,512]{2,1,0:T(8,128)(2,1)}), bf16[2,768,2048]{2,1,0:T(8,128)(2,1)}) %all-gather.5.cloned.1.call-update) | async-done | bytes 6291472 | tf_op jit(solution)/shard_map/all_gather | solution.py:34
  127.7 6.3 %fusion.2 = f32[8,2,36]{2,0,1:T(8,128)S(1)} fusion(bf16[8,2,36,2048]{3,1,2,0:T(2,128)(2,1)S(1)} %all-to-all-done, bf16[2,768,2048]{2,1,0:T(8,128)(2,1)} %all-gather.5.cloned.1.call-done, bf16[8,2,36,768]{3,1,2,0:T(2,128)(2,1)S(1)} %bitcast.46), kind=kOutput, calls=%fused_computation.5 | convolution fusion | flops 1817837056 | bytes 9537792 | tf_op jit(solution)/shard_map/secf,efn->secn/dot_general | solution.py:31
  134.0 0.6 copy.66
  134.6 3.8 %all-to-all-start.1 = ((f32[8,2,36]{2,1,0:T(2,128)}), f32[8,2,36]{2,1,0:T(2,128)S(1)}, u32[]{:S(2)}, u32[]{:S(2)}) async-start(f32[8,2,36]{2,1,0:T(2,128)} %copy.66), calls=%async_computation.1 | async-start | bytes 16384 | tf_op jit(solution)/shard_map/all_to_all | solution.py:38
  138.5 0.1 copy.68
  138.6 4.6 %all-to-all-done.1 = f32[8,2,36]{2,1,0:T(2,128)S(1)} async-done(((f32[8,2,36]{2,1,0:T(2,128)}), f32[8,2,36]{2,1,0:T(2,128)S(1)}, u32[]{:S(2)}, u32[]{:S(2)}) %all-to-all-start.1) | async-done | bytes 2336 | tf_op jit(solution)/shard_map/all_to_all | solution.py:38
  143.3 2.3 %gather_fusion = f32[512]{0:T(512)S(1)} fusion(f32[576]{0:T(1024)S(1)} %reshape.76, s32[1024]{0:T(1024)S(1)} %pad_clamp_fusion), kind=kCustom, calls=%fused_computation | custom fusion | bytes 6144 | tf_op jit(solution)/shard_map/gather | solution.py:39
  145.6 0.1 reshape.77
  145.7 0.1 multiply_reduce_fusion
  146.0 0.6 stack.2
  146.6 3.3 %all-to-all-start.2 = ((bf16[4,128,16]{1,2,0:T(8,128)(2,1)}), bf16[4,128,16]{1,2,0:T(8,128)(2,1)S(1)}, u32[]{:S(2)}, u32[]{:S(2)}) async-start(bf16[4,128,16]{1,2,0:T(8,128)(2,1)} %stack.2), calls=%async_computation.2 | async-start | bytes 32768 | tf_op jit(solution)/shard_map/all_to_all | solution.py:46
  149.8 23.6 %all-gather.3.cloned.1.call-done = bf16[512,2048]{1,0:T(8,128)(2,1)} async-done(((bf16[128,2048]{1,0:T(8,128)(2,1)}), bf16[512,2048]{1,0:T(8,128)(2,1)}) %all-gather.3.cloned.1.call-update) | async-done | bytes 2097168 | tf_op jit(solution)/shard_map/all_gather | solution.py:21
  173.5 2.5 %add_convert_fusion = bf16[512,2048]{1,0:T(8,128)(2,1)S(1)} fusion(bf16[512,2048]{1,0:T(8,128)(2,1)} %all-gather.3.cloned.1.call-done, bf16[2048,16]{0,1:T(8,128)(2,1)S(1)} %copy-done.2, bf16[4,128,16]{1,2,0:T(8,128)(2,1)S(1)} %all-to-all-done.2), kind=kOutput, calls=%fused_computation.6 | convolution fusion | flops 36700160 | bytes 4276224 | tf_op jit(solution)/shard_map/dot_general | solution.py:56
  175.9 0.3 copy-done.6
  176.3 3.3 %convolution_convert_fusion = bf16[512,1024]{1,0:T(8,128)(2,1)} fusion(bf16[512,2048]{1,0:T(8,128)(2,1)S(1)} %add_convert_fusion, bf16[1024,2048]{1,0:T(8,128)(2,1)S(1)} %copy-done.6), kind=kOutput, calls=%fused_computation.8 | convolution fusion | flops 2148007936 | bytes 7340032 | tf_op jit(solution)/shard_map/dot_general | solution.py:60
  (26 shorter events, 0.5 us)
Async XLA Ops:
  7.2 120.5 %copy-start = (bf16[1,8,2,36,768]{4,2,3,1,0:T(2,128)(2,1)S(1)}, bf16[1,8,2,36,768]{4,2,3,1,0:T(2,128)(2,1)}, u32[]{:S(2)}) copy-start(bf16[1,8,2,36,768]{4,2,3,1,0:T(2,128)(2,1)} %param.10) | copy-start | bytes 2654212
  7.2 4.1 %copy-start.1 = (bf16[128,2048]{1,0:T(8,128)(2,1)S(1)}, bf16[128,2048]{1,0:T(8,128)(2,1)}, u32[]{:S(2)}) copy-start(bf16[128,2048]{1,0:T(8,128)(2,1)} %param.7) | copy-start | bytes 1572868
  7.2 120.5 %all-gather.5.cloned.1.call-start = ((), (), s32[]{:S(2)}) async-start(), calls=%async_computation.4 | async-start | bytes 7864320 | tf_op jit(solution)/shard_map/all_gather | solution.py:34
  27.5 34.6 %all-to-all-start = ((bf16[8,2,36,2048]{3,1,2,0:T(2,128)(2,1)}), bf16[8,2,36,2048]{3,1,2,0:T(2,128)(2,1)S(1)}, u32[]{:S(2)}, u32[]{:S(2)}) async-start(bf16[8,2,36,2048]{3,1,2,0:T(2,128)(2,1)} %copy.63), calls=%async_computation | async-start | bytes 4718592 | tf_op jit(solution)/shard_map/all_to_all | solution.py:30
  32.7 140.8 %all-gather.3.cloned.1.call-start = ((), (), s32[]{:S(2)}) async-start(), calls=%async_computation.3 | async-start | bytes 2621440 | tf_op jit(solution)/shard_map/all_gather | solution.py:21
  127.7 10.8 %copy-start.5 = (f32[128,4]{0,1:T(4,128)S(1)}, f32[128,4]{0,1:T(4,128)}, u32[]{:S(2)}) copy-start(f32[128,4]{0,1:T(4,128)} %param.9) | copy-start | bytes 6148
  134.0 11.9 %copy-start.3 = (s32[128,4]{0,1:T(4,128)S(1)}, s32[128,4]{0,1:T(4,128)}, u32[]{:S(2)}) copy-start(s32[128,4]{0,1:T(4,128)} %param.8) | copy-start | bytes 6148
  134.0 39.4 %copy-start.2 = (bf16[2048,16]{0,1:T(8,128)(2,1)S(1)}, bf16[2048,16]{0,1:T(8,128)(2,1)}, u32[]{:S(2)}) copy-start(bf16[2048,16]{0,1:T(8,128)(2,1)} %param.12) | copy-start | bytes 196612
  134.6 8.5 %all-to-all-start.1 = ((f32[8,2,36]{2,1,0:T(2,128)}), f32[8,2,36]{2,1,0:T(2,128)S(1)}, u32[]{:S(2)}, u32[]{:S(2)}) async-start(f32[8,2,36]{2,1,0:T(2,128)} %copy.66), calls=%async_computation.1 | async-start | bytes 16384 | tf_op jit(solution)/shard_map/all_to_all | solution.py:38
  145.9 33.7 %copy-start.4 = (f32[128,4]{0,1:T(4,128)}, f32[128,4]{0,1:T(4,128)S(1)}, u32[]{:S(2)}) copy-start(f32[128,4]{0,1:T(4,128)S(1)} %copy.69) | copy-start | bytes 6148
  146.6 26.9 %all-to-all-start.2 = ((bf16[4,128,16]{1,2,0:T(8,128)(2,1)}), bf16[4,128,16]{1,2,0:T(8,128)(2,1)S(1)}, u32[]{:S(2)}, u32[]{:S(2)}) async-start(bf16[4,128,16]{1,2,0:T(8,128)(2,1)} %stack.2), calls=%async_computation.2 | async-start | bytes 32768 | tf_op jit(solution)/shard_map/all_to_all | solution.py:46
  173.4 2.8 %copy-start.6 = (bf16[1024,2048]{1,0:T(8,128)(2,1)S(1)}, bf16[1024,2048]{1,0:T(8,128)(2,1)}, u32[]{:S(2)}) copy-start(bf16[1024,2048]{1,0:T(8,128)(2,1)} %param.13) | copy-start | bytes 12582916
Sparse Core Ops, SparseCore 0:
  9.6 118.0 all-gather.4
  129.2 44.1 all-gather.2
